TPU v7x, 32 devices: a whole 2x2x4 slice. The times are simulated.
32 devices in a mesh: replica: 2 (over y), tensor: 16 (over z, x, core).
Axes of the slice: x: 2, y: 2, z: 4, core: 2. Of those that a mesh axis runs over, the one named last changes fastest.
Arguments:
- tokens: bfloat16 [256, 2560], P('replica', 'tensor'), may hold values from -6 to 6
- next_tokens: bfloat16 [128, 2560], P('replica', 'tensor'), may hold values from -6 to 6
- cotangent: bfloat16 [256, 2560], P('replica', 'tensor'), may hold values from -0.5 to 0.5
- gate_weight: bfloat16 [2560, 14336], P(None, 'tensor'), may hold values from -0.125 to 0.125
- up_weight: bfloat16 [2560, 14336], P(None, 'tensor'), may hold values from -0.125 to 0.125
- down_weight: bfloat16 [14336, 2560], P('tensor'), may hold values from -0.046875 to 0.046875
- momentum: bfloat16 [2, 14336, 2560], P('replica', 'tensor'), may hold values from -6 to 6
- indices: int32 [2, 224, 40, 32], P(None, 'tensor'), may hold values from 0 to 4095, as said below
Outputs:
- output: bfloat16 [128, 2560], P(('replica', 'tensor'))
- new_momentum: bfloat16 [2, 14336, 2560], P('replica', 'tensor')
Inputs may be any that keep to these rules, and one draw needn't show every extreme that they name: Within one replica and tile the 32 indices are distinct; the n-th lies in the range from n * 64 * 2 to (n + 1) * 64 * 2 - 1.
All inputs are finite; a program needn't handle non-finite values.
Results may differ from a plain program's by a relative error of at most 0.017.
Values may be sent and summed in bfloat16 or wider, within the bound.
A program may use at most 128 MiB of HBM per device.

v0:
```python
import functools

import jax
import jax.numpy as jnp
import numpy as np
from jax import lax
from jax.experimental import pallas as pl
from jax.experimental.pallas import tpu as pltpu
from jax.sharding import PartitionSpec as P

TILE = 64
BETA_DECAY = 0.9
STEP_RATE = 0.1
MESH = pl.DeviceIdType.MESH
VMEM = pl.BlockSpec(memory_space=pltpu.VMEM)


def cosine_table():
    freq = np.arange(TILE)[:, None]
    place = np.arange(TILE)[None, :]
    table = np.cos(np.pi * (2.0 * place + 1.0) * freq / (2.0 * TILE))
    return table * np.where(freq == 0, np.sqrt(1.0 / TILE), np.sqrt(2.0 / TILE))


def split_bf16(table):
    high = jnp.asarray(table, jnp.float32).astype(jnp.bfloat16)
    rest = jnp.asarray(table, jnp.float32) - high.astype(jnp.float32)
    return high, rest.astype(jnp.bfloat16)


def tables(strip, chunk):
    table = cosine_table()
    across = np.kron(np.eye(chunk // TILE), table)
    down = np.concatenate(
        [np.kron(np.eye(strip), table[0::2]), np.kron(np.eye(strip), table[1::2])], axis=0
    )
    row_high, row_low = split_bf16(down)
    col_high, col_low = split_bf16(across.T)
    row = jnp.concatenate([row_high, row_low], axis=1)
    inverse_row = jnp.asarray(down.T, jnp.float32).astype(jnp.bfloat16)
    inverse_col = jnp.asarray(across, jnp.float32).astype(jnp.bfloat16)
    return row, col_high, col_low, inverse_row, inverse_col


def flip(index, bits):
    bit = 1
    while bit <= bits:
        if bits & bit:
            index = index + bit - 2 * bit * ((index // bit) % 2)
        bit *= 2
    return index


def greet(axis, others):
    barrier = pltpu.get_barrier_semaphore()
    for other in others:
        pl.semaphore_signal(barrier, inc=1, device_id={axis: other}, device_id_type=MESH)
    pl.semaphore_wait(barrier, len(others))


def hidden_kernel(
    size, feature_block, grad_block, gate_weight, up_weight, grads, hidden, next_hidden,
    held, features, turned, gate, upper, send, recv, local,
):
    me = lax.axis_index("tensor")
    depth = size // 4
    z, x, core = me // 4, (me // 2) % 2, me % 2
    blocks, kept = (feature_block, grad_block), (held, grads)

    def slot(zz, xx, cc):
        return (zz * 2 + xx) * 2 + cc

    loads = [
        pltpu.make_async_copy(source, target, local.at[n])
        for n, (source, target) in enumerate(
            [
                (feature_block, held.at[me]),
                (grad_block, grads.at[me]),
                (gate_weight, gate),
                (up_weight, upper),
            ]
        )
    ]
    for load in loads:
        load.start()
    others = [flip(z, k) for k in range(1, depth)]
    side, twin = slot(z, 1 - x, core), slot(z, x, 1 - core)
    greet("tensor", [slot(zz, x, core) for zz in others] + [side, twin])
    copies = []

    def push(kind, which, target, source=None):
        copy = pltpu.make_async_remote_copy(
            src_ref=kept[kind].at[which] if source is None else source,
            dst_ref=kept[kind].at[which],
            send_sem=send.at[len(copies)],
            recv_sem=recv.at[kind, which],
            device_id={"tensor": target},
            device_id_type=MESH,
        )
        copy.start()
        copies.append(copy)

    def arrive(kind, which):
        pltpu.make_async_remote_copy(
            src_ref=blocks[kind],
            dst_ref=kept[kind].at[which],
            send_sem=send.at[0],
            recv_sem=recv.at[kind, which],
            device_id={"tensor": twin},
            device_id_type=MESH,
        ).wait_recv()

    for kind in range(2):
        for target in [side] + [slot(zz, x, core) for zz in others] + [twin]:
            push(kind, me, target, blocks[kind])
    for kind in range(2):
        for zz in others:
            which = slot(zz, x, core)
            arrive(kind, which)
            push(kind, which, side)
            push(kind, which, twin)
    for kind in range(2):
        for zz in [z] + others:
            which = slot(zz, 1 - x, core)
            arrive(kind, which)
            push(kind, which, twin)
    for load in loads:
        load.wait()
    for zz in [z] + others:
        arrive(0, slot(zz, x, 1 - core))
        arrive(0, slot(zz, 1 - x, 1 - core))
    share, count = grads.shape[1:]
    nexts = next_hidden.shape[1]
    split = share // 2
    for n in range(size):
        base = n * share
        features[base : base + share, :count] = held[n, :share]
        features[base : base + split, count:] = held[n, share:, :nexts]
        features[base + split : base + share, count:] = held[n, share:, nexts:]
    turned[...] = features[...].T
    wide = dot(turned[...], gate[...])
    mixed = (wide / (1.0 + jnp.exp(-wide)) * dot(turned[...], upper[...])).astype(jnp.bfloat16).T
    hidden[...] = mixed[:, :count]
    next_hidden[...] = mixed[:, count:]
    for zz in [z] + others:
        arrive(1, slot(zz, x, 1 - core))
        arrive(1, slot(zz, 1 - x, 1 - core))
    for copy in copies:
        copy.wait_send()


def hidden_pass(feature_block, grad_block, gate_weight, up_weight, nexts, size):
    share, count = grad_block.shape
    breadth, width = gate_weight.shape
    kind = jnp.bfloat16
    hbm = pl.BlockSpec(memory_space=pl.ANY)
    return pl.pallas_call(
        functools.partial(hidden_kernel, size),
        out_shape=(
            jax.ShapeDtypeStruct((size, share, count), kind),
            jax.ShapeDtypeStruct((width, count), kind),
            jax.ShapeDtypeStruct((width, nexts), kind),
        ),
        in_specs=[VMEM, VMEM, hbm, hbm],
        out_specs=(VMEM, VMEM, VMEM),
        scratch_shapes=[
            pltpu.VMEM((size,) + feature_block.shape, kind),
            pltpu.VMEM((breadth, count + nexts), kind),
            pltpu.VMEM((count + nexts, breadth), kind),
            pltpu.VMEM(gate_weight.shape, kind),
            pltpu.VMEM(up_weight.shape, kind),
            pltpu.SemaphoreType.DMA((2 * size,)),
            pltpu.SemaphoreType.DMA((2, size)),
            pltpu.SemaphoreType.DMA((4,)),
        ],
        compiler_params=pltpu.CompilerParams(collective_id=0, has_side_effects=True),
        name="hidden_pass",
    )(feature_block, grad_block, gate_weight, up_weight)


def dot(a, b):
    return jnp.dot(a, b, preferred_element_type=jnp.float32)


def contract(a, b, dim):
    return lax.dot_general(
        a, b, (((dim,), (dim,)), ((), ())), preferred_element_type=jnp.float32
    )


def lanes(shape):
    return lax.broadcasted_iota(jnp.int32, shape, 1) % TILE


def strip_offsets(indices, which):
    strip, keep, columns = indices.shape[1:]
    first = lax.broadcasted_iota(jnp.int32, (keep, columns), 0) * (TILE * TILE // keep)
    listed = [
        (indices[which, n] - first).astype(jnp.float32).astype(jnp.bfloat16) for n in range(strip)
    ]
    return jnp.concatenate(listed, axis=0)


def moment_kernel(
    chunk, hidden, grads, momentum, indices, spread, gather, row, col_high, col_low,
    inverse_row, inverse_col, kept, mine, sent,
    moment, mixed, offset, picked, stacked, pair,
):
    tall, breadth = moment.shape
    half = tall // 2
    spans = [slice(start, start + chunk) for start in range(0, breadth, chunk)]
    own_offsets = strip_offsets(indices, lax.axis_index("replica"))
    for span in spans:
        offset[:, span] = dot(own_offsets, spread[:, span])
    for span in spans:
        moment[:, span] = BETA_DECAY * momentum[0, :, span].astype(jnp.float32) + contract(
            hidden[...], grads[span, :], 1
        )
    for k, span in enumerate(spans):
        rounded = moment[:, span].astype(jnp.bfloat16)
        mixed[k * tall : (k + 1) * tall] = dot(
            row[...], jnp.concatenate([rounded, rounded], axis=0)
        ).astype(jnp.bfloat16)
    place = lanes((half, chunk)).astype(jnp.float32)
    for k, span in enumerate(spans):
        part = mixed[k * tall : (k + 1) * tall]
        spectrum = dot(part, col_high[...]) + dot(part, col_low[...])
        where = offset[:, span]
        values = jnp.where(
            where == place,
            spectrum[:half],
            jnp.where(where == place + TILE, spectrum[half:], 0.0),
        ).astype(jnp.bfloat16)
        picked[:, span] = values
        stacked[k * half : (k + 1) * half] = values
    sent[...] = dot(picked[...], gather[...]).astype(jnp.bfloat16)
    for k, span in enumerate(spans):
        wide = dot(stacked[k * half : (k + 1) * half], inverse_col[...])
        odd = offset[:, span] >= TILE
        pair[:half, span] = jnp.where(odd, 0.0, wide).astype(jnp.bfloat16)
        pair[half:, span] = jnp.where(odd, wide, 0.0).astype(jnp.bfloat16)
    for span in spans:
        own = dot(inverse_row[...], pair[:, span])
        kept[0, :, span] = (moment[:, span] - own).astype(jnp.bfloat16)
        mine[:, span] = own.astype(jnp.bfloat16)


def whole_block(array):
    return pl.BlockSpec(array.shape, lambda i: (0,) * array.ndim)


def moment_pass(hidden, grads, momentum, indices, spread, mats, strip, chunk):
    rows, breadth = momentum.shape[1:]
    tall = strip * TILE
    replicas, _, keep, columns = indices.shape
    half = strip * keep
    row, col_high, col_low, inverse_row, inverse_col = mats
    gather = spread.T
    return pl.pallas_call(
        functools.partial(moment_kernel, chunk),
        grid=(rows // tall,),
        out_shape=(
            jax.ShapeDtypeStruct((1, rows, breadth), jnp.bfloat16),
            jax.ShapeDtypeStruct((rows, breadth), jnp.bfloat16),
            jax.ShapeDtypeStruct((rows // 2, columns), jnp.bfloat16),
        ),
        in_specs=[
            pl.BlockSpec((tall, hidden.shape[1]), lambda i: (i, 0)),
            whole_block(grads),
            pl.BlockSpec((1, tall, breadth), lambda i: (0, i, 0)),
            pl.BlockSpec((replicas, strip, keep, columns), lambda i: (0, i, 0, 0)),
            whole_block(spread),
            whole_block(gather),
            whole_block(row),
            whole_block(col_high),
            whole_block(col_low),
            whole_block(inverse_row),
            whole_block(inverse_col),
        ],
        out_specs=(
            pl.BlockSpec((1, tall, breadth), lambda i: (0, i, 0)),
            pl.BlockSpec((tall, breadth), lambda i: (i, 0)),
            pl.BlockSpec((half, columns), lambda i: (i, 0)),
        ),
        scratch_shapes=[
            pltpu.VMEM((tall, breadth), jnp.float32),
            pltpu.VMEM((tall * (breadth // chunk), chunk), jnp.bfloat16),
            pltpu.VMEM((half, breadth), jnp.float32),
            pltpu.VMEM((half, breadth), jnp.bfloat16),
            pltpu.VMEM((half * (breadth // chunk), chunk), jnp.bfloat16),
            pltpu.VMEM((tall, breadth), jnp.bfloat16),
        ],
        name="moment_pass",
    )(
        hidden, grads, momentum, indices, spread, gather, row, col_high, col_low, inverse_row,
        inverse_col,
    )


def output_kernel(
    chunk, size, hidden, down, mine, values, indices, spread, inverse_row, inverse_col,
    out, placed, wide, new, stage, held, send, recv, offset, received, pass_send, pass_recv,
):
    step = pl.program_id(0)
    steps = stage.shape[0]
    replicas = indices.shape[0]
    rows, breadth = new.shape
    tall = inverse_row.shape[0]
    half = tall // 2
    strips = rows // tall
    spans = [slice(start, start + chunk) for start in range(0, breadth, chunk)]
    replica = lax.axis_index("replica")
    me = lax.axis_index("tensor")
    barrier = pltpu.get_barrier_semaphore()

    def share(k):
        return pltpu.make_async_remote_copy(
            src_ref=values,
            dst_ref=received.at[k - 1],
            send_sem=pass_send.at[k - 1],
            recv_sem=pass_recv.at[k - 1],
            device_id={"replica": (replica - k + replicas) % replicas},
            device_id_type=MESH,
        )

    @pl.when(step == 0)
    def _():
        for k in range(1, size):
            pl.semaphore_signal(
                barrier, inc=1, device_id={"tensor": (me + k) % size}, device_id_type=MESH
            )
        for k in range(1, replicas):
            pl.semaphore_signal(
                barrier, inc=1, device_id={"replica": (replica + k) % replicas},
                device_id_type=MESH,
            )
        pl.semaphore_wait(barrier, size + replicas - 2)
        for k in range(1, replicas):
            share(k).start()

    place = lanes((rows // 2, chunk)).astype(jnp.float32)
    listed = [strip_offsets(indices, (replica + k) % replicas) for k in range(1, replicas)]
    for k in range(replicas - 1):
        offset[k] = dot(listed[k], spread[...])

    @pl.when(step == 0)
    def _():
        for k in range(1, replicas):
            share(k).wait()

    for n, span in enumerate(spans):
        even = odd = 0.0
        for k in range(replicas - 1):
            where = offset[k, :, span]
            value = dot(received[k], spread[:, span])
            even = even + jnp.where(where == place, value, 0.0)
            odd = odd + jnp.where(where == place + TILE, value, 0.0)
        even, odd = even.astype(jnp.bfloat16), odd.astype(jnp.bfloat16)
        for m in range(strips):
            base = n * rows + m * tall
            placed[base : base + half] = even[m * half : (m + 1) * half]
            placed[base + half : base + tall] = odd[m * half : (m + 1) * half]
    for n, span in enumerate(spans):
        wide[:, span] = dot(placed[n * rows : (n + 1) * rows], inverse_col[...]).astype(
            jnp.bfloat16
        )
    for m in range(strips):
        band = slice(m * tall, (m + 1) * tall)
        update = mine[band].astype(jnp.float32) + dot(inverse_row[...], wide[band])
        new[band] = (
            down[band].astype(jnp.float32) - (STEP_RATE / replicas) * update
        ).astype(jnp.bfloat16)
    part = contract(hidden[...], new[...], 0).astype(jnp.bfloat16)
    short = out.shape[0]
    for n in range(size):
        stage[step, n] = part[n * short : (n + 1) * short]

    def transfer(which, k):
        target = (me + k) % size
        return pltpu.make_async_remote_copy(
            src_ref=stage.at[which, target],
            dst_ref=held.at[which, k - 1],
            send_sem=send.at[which, k - 1],
            recv_sem=recv.at[which, k - 1],
            device_id={"tensor": target},
            device_id_type=MESH,
        )

    for k in range(1, size):
        transfer(step, k).start()

    @pl.when(step == steps - 1)
    def _():
        for which in range(steps):
            total = stage[which, me].astype(jnp.float32)
            for k in range(1, size):
                transfer(which, k).wait()
                total = total + held[which, k - 1].astype(jnp.float32)
            out[:, which * breadth : (which + 1) * breadth] = total.astype(out.dtype)


def output_pass(hidden, down, mine, values, indices, spread, mats, chunk, size):
    rows, breadth = down.shape
    columns = spread.shape[0]
    part = 2 * chunk if breadth % (2 * chunk) == 0 else chunk
    steps = breadth // part
    short = hidden.shape[1] // size
    inverse_row, inverse_col = mats[3:]
    kind = jnp.bfloat16
    return pl.pallas_call(
        functools.partial(output_kernel, chunk, size),
        grid=(steps,),
        out_shape=jax.ShapeDtypeStruct((short, breadth), kind),
        in_specs=[
            whole_block(hidden),
            pl.BlockSpec((rows, part), lambda i: (0, i)),
            pl.BlockSpec((rows, part), lambda i: (0, i)),
            whole_block(values),
            whole_block(indices),
            pl.BlockSpec((columns, part), lambda i: (0, i)),
            whole_block(inverse_row),
            whole_block(inverse_col),
        ],
        out_specs=pl.BlockSpec((short, breadth), lambda i: (0, 0)),
        scratch_shapes=[
            pltpu.VMEM((rows * (part // chunk), chunk), kind),
            pltpu.VMEM((rows, part), kind),
            pltpu.VMEM((rows, part), kind),
            pltpu.VMEM((steps, size, short, part), kind),
            pltpu.VMEM((steps, size - 1, short, part), kind),
            pltpu.SemaphoreType.DMA((steps, size - 1)),
            pltpu.SemaphoreType.DMA((steps, size - 1)),
            pltpu.VMEM((indices.shape[0] - 1, rows // 2, part), jnp.float32),
            pltpu.VMEM((indices.shape[0] - 1,) + values.shape, kind),
            pltpu.SemaphoreType.DMA((indices.shape[0] - 1,)),
            pltpu.SemaphoreType.DMA((indices.shape[0] - 1,)),
        ],
        compiler_params=pltpu.CompilerParams(collective_id=2, has_side_effects=True),
        name="output_pass",
    )(hidden, down, mine, values, indices, spread, inverse_row, inverse_col)


def on_device(
    tokens, next_tokens, cotangent, gate_weight, up_weight, down_weight, momentum, indices
):
    size = lax.axis_size("tensor")
    replicas = lax.axis_size("replica")
    count, share = tokens.shape
    nexts = next_tokens.shape[0]
    breadth = share * size
    tile_rows, tile_cols, keep = indices.shape[1:]
    strip = next(n for n in (4, 2, 1) if tile_rows % n == 0)
    chunk = next(n for n in (256, 128) if breadth % n == 0)

    turned = next_tokens.T
    block = jnp.concatenate(
        [tokens.T, jnp.concatenate([turned[: share // 2], turned[share // 2 :]], axis=1)], axis=0
    )
    grads, hidden, next_hidden = hidden_pass(
        block, cotangent.T, gate_weight, up_weight, nexts, size
    )
    grads = grads.reshape(breadth, count)
    indices = jnp.swapaxes(indices, 2, 3)
    spread = jnp.asarray(np.kron(np.eye(tile_cols), np.ones((1, TILE))), jnp.bfloat16)
    mats = tables(strip, chunk)
    kept, mine, values = moment_pass(
        hidden, grads, momentum, indices, spread, mats, strip, chunk
    )
    output = output_pass(
        next_hidden, down_weight, mine, values, indices, spread, mats, chunk, size
    )
    return (output, kept)


def solution(mesh):
    return jax.shard_map(
        on_device,
        mesh=mesh,
        in_specs=(
            P("replica", "tensor"),
            P("replica", "tensor"),
            P("replica", "tensor"),
            P(None, "tensor"),
            P(None, "tensor"),
            P("tensor", None),
            P("replica", "tensor", None),
            P(None, "tensor", None, None),
        ),
        out_specs=(P(("replica", "tensor"), None), P("replica", "tensor", None)),
        check_vma=False,
    )
```

profile of v0, /device:TPU:0, one launch (start us, length us, event | category | flops | bytes accessed | tf_op | source)
XLA Modules:
  0.0 64.9 jit_solution(5116735013314094810)
XLA Ops:
  0.6 0.9 %copy.17 = bf16[64,160]{0,1:T(8,128)(2,1)S(1)} copy(bf16[64,160]{1,0:T(8,128)(2,1)} %param.16) | data formatting | bytes 40960 | tf_op args[1]
  1.5 1.5 %maximum_maximum_fusion.feature_block = bf16[240,128]{1,0:T(8,128)(2,1)} fusion(bf16[80,64]{1,0:T(8,128)(2,1)S(1)} %get-tuple-element.15, bf16[80,64]{1,0:T(8,128)(2,1)S(1)} %get-tuple-element.14, bf16[160,128]{1,0:T(8,128)(2,1)} %bitcast.9), kind=kLoop, calls=%fused_computation | loop fusion | flops 184320 | bytes 122880 | tf_op jit(solution)/shard_map/concatenate | solution.py:456
  3.0 23.8 %hidden_pass.1 = (bf16[16,160,128]{2,1,0:T(8,128)(2,1)}, bf16[896,128]{1,0:T(8,128)(2,1)}, bf16[896,64]{1,0:T(8,128)(2,1)}) custom-call(bf16[240,128]{1,0:T(8,128)(2,1)} %maximum_maximum_fusion.feature_block, bf16[160,128]{1,0:T(8,128)(2,1)} %bitcast.10, bf16[2560,896]{1,0:T(8,128)(2,1)} %gate_weight.1, bf16[2560,896]{1,0:T(8,128)(2,1)} %up_weight.1), custom_call_target="tpu_custom_call" | custom-call | tf_op jit(solution)/shard_map/hidden_pass/pallas_call | solution.py:157
  26.8 14.6 %moment_pass.1 = (bf16[1,896,2560]{2,1,0:T(8,128)(2,1)}, bf16[896,2560]{1,0:T(8,128)(2,1)}, bf16[448,40]{1,0:T(8,128)(2,1)}) custom-call(bf16[896,128]{1,0:T(8,128)(2,1)} %get-tuple-element.9.hidden, bf16[2560,128]{1,0:T(8,128)(2,1)} %bitcast.7, bf16[1,896,2560]{2,1,0:T(8,128)(2,1)} %momentum.1, s32[2,14,32,40]{3,2,1,0:T(8,128)} %bitcast.5, ...), custom_call_target="tpu_custom_call" | custom-call | tf_op jit(solution)/shard_map/moment_pass/pallas_call | solution.py:259
  41.4 22.1 %output_pass.1 = bf16[4,2560]{1,0:T(4,128)(2,1)} custom-call(bf16[896,64]{1,0:T(8,128)(2,1)} %get-tuple-element.8.hidden, bf16[896,2560]{1,0:T(8,128)(2,1)} %down.1, bf16[896,2560]{1,0:T(8,128)(2,1)} %get-tuple-element.11.mine, bf16[448,40]{1,0:T(8,128)(2,1)} %get-tuple-element.12.values, s32[2,14,32,40]{3,2,1,0:T(8,128)} %bitcast.6, ...), custom_call_target="tpu_custom_call" | custom-call | tf_op jit(solution)/shard_map/output_pass/pallas_call | solution.py:410
  63.6 1.3 %copy.19 = bf16[4,2560]{1,0:T(4,128)(2,1)} copy(bf16[4,2560]{1,0:T(4,128)(2,1)} %output_pass.1) | data formatting | bytes 40960
  (1 shorter events, 0.0 us)
where the time goes:
time: 65.4 us; the launch traced here: 64.9 us
  Pallas kernels  60.5 us (93%)
  local copies, waits for them, and re-layouts  2.21 us (3%)
  other arithmetic  1.49 us (2%)
  between operations  0.66 us (1%)
    pallas_call x1, Pallas kernels, hidden_pass(): pl.pallas_call(functools.partial(hidden_kernel, size), out_shape=(jax.Sha...  23.8 us
    pallas_call x1, Pallas kernels, output_pass(): pl.pallas_call(functools.partial(output_kernel, chunk, size), grid=(steps...  22.1 us
    pallas_call x1, Pallas kernels, moment_pass(): pl.pallas_call(functools.partial(moment_kernel, chunk), grid=(rows // tal...  14.6 us
    unnamed x2, local copies, waits for them, and re-layouts  2.21 us
    concatenate x1, other arithmetic, on_device(): jnp.concatenate([tokens.T, jnp.concatenate([turned[:share // 2], turned[s...  1.49 us

commit v1 on v0

v1 whole, which is shorter than its diff:
```python
import functools

import jax
import jax.numpy as jnp
import numpy as np
from jax import lax
from jax.experimental import pallas as pl
from jax.experimental.pallas import tpu as pltpu
from jax.sharding import PartitionSpec as P

TILE = 64
BETA_DECAY = 0.9
STEP_RATE = 0.1
MESH = pl.DeviceIdType.MESH
ANY = pl.BlockSpec(memory_space=pl.ANY)
VMEM = pl.BlockSpec(memory_space=pltpu.VMEM)
KIND = jnp.bfloat16


def cosine_table():
    freq = np.arange(TILE)[:, None]
    place = np.arange(TILE)[None, :]
    table = np.cos(np.pi * (2.0 * place + 1.0) * freq / (2.0 * TILE))
    return table * np.where(freq == 0, np.sqrt(1.0 / TILE), np.sqrt(2.0 / TILE))


def split_bf16(table):
    high = jnp.asarray(table, jnp.float32).astype(KIND)
    rest = jnp.asarray(table, jnp.float32) - high.astype(jnp.float32)
    return high, rest.astype(KIND)


def halves(count):
    table = cosine_table()
    eye = np.eye(count)
    return np.concatenate([np.kron(eye, table[0::2]), np.kron(eye, table[1::2])], axis=0)


def flip(index, bits):
    bit = 1
    while bit <= bits:
        if bits & bit:
            index = index + bit - 2 * bit * ((index // bit) % 2)
        bit *= 2
    return index


def dot(a, b):
    return jnp.dot(a, b, preferred_element_type=jnp.float32)


def contract(a, b, dim):
    return lax.dot_general(
        a, b, (((dim,), (dim,)), ((), ())), preferred_element_type=jnp.float32
    )


def strip_offsets(indices, which):
    tiles, keep, columns = indices.shape[1:]
    first = lax.broadcasted_iota(jnp.int32, (keep, columns), 0) * (TILE * TILE // keep)
    listed = [
        (indices[which, n] - first).astype(jnp.float32).astype(KIND) for n in range(tiles)
    ]
    return jnp.concatenate(listed, axis=0)


def step_kernel(
    size, replicas, strip, chunk, wide,
    tok, nxt, cot, gate_hbm, upper_hbm, down_hbm, momentum_hbm, indices_hbm,
    row_hbm, turn_hbm, across_hbm, order_hbm,
    out, hidden, grads, pair, momentum,
    nxt_in, held_tok, held_nxt, held_cot,
    gate, upper, down, indices, spread, gather, row, turn, across, order,
    features, basis, early, mine, theirs, total,
    stage_core, held_core, stage_side, held_side, stage_deep, held_deep, split_sum,
    send, recv, local, pass_send, pass_recv, fold_send, fold_recv, deep_send, deep_recv,
):
    depth = size // 4
    me = lax.axis_index("tensor")
    replica = lax.axis_index("replica")
    z, x, core = me // 4, (me // 2) % 2, me % 2
    share, count = tok.shape
    nexts = nxt.shape[0]
    rows, breadth = down.shape
    half = rows // 2
    split = share // 2
    group = 4 * share
    blocks, kept = (tok, held_nxt.at[me], cot), (held_tok, held_nxt, held_cot)

    def slot(zz, xx, cc):
        return (zz * 2 + xx) * 2 + cc

    names = [
        (nxt, nxt_in), (order_hbm, order), (indices_hbm, indices), (across_hbm, across),
        (tok, held_tok.at[me]), (gate_hbm, gate), (upper_hbm, upper), (row_hbm, row),
        (turn_hbm, turn), (momentum_hbm.at[0], momentum), (cot, held_cot.at[me]), (down_hbm, down),
    ]
    loads = [
        pltpu.make_async_copy(source, target, local.at[n])
        for n, (source, target) in enumerate(names)
    ]
    for load in loads:
        load.start()

    others = [flip(z, k) for k in range(1, depth)]
    deep = [slot(zz, x, core) for zz in others]
    side, twin = slot(z, 1 - x, core), slot(z, x, 1 - core)
    barrier = pltpu.get_barrier_semaphore()
    for target in deep + [side, twin]:
        pl.semaphore_signal(barrier, inc=1, device_id={"tensor": target}, device_id_type=MESH)
    for k in range(1, replicas):
        pl.semaphore_signal(
            barrier, inc=1, device_id={"replica": (replica + k) % replicas}, device_id_type=MESH
        )
    ribbon = spread.shape
    spread[...] = jnp.where(
        lax.broadcasted_iota(jnp.int32, ribbon, 1) // TILE
        == lax.broadcasted_iota(jnp.int32, ribbon, 0),
        1.0,
        0.0,
    ).astype(KIND)
    gather[...] = spread[...].T
    pl.semaphore_wait(barrier, depth + replicas)

    copies = []

    def push(kind, which, target, source=None):
        copy = pltpu.make_async_remote_copy(
            src_ref=kept[kind].at[which] if source is None else source,
            dst_ref=kept[kind].at[which],
            send_sem=send.at[len(copies)],
            recv_sem=recv.at[kind, which],
            device_id={"tensor": target},
            device_id_type=MESH,
        )
        copy.start()
        copies.append(copy)

    def arrive(kind, which):
        pltpu.make_async_remote_copy(
            src_ref=blocks[kind],
            dst_ref=kept[kind].at[which],
            send_sem=send.at[0],
            recv_sem=recv.at[kind, which],
            device_id={"tensor": twin},
            device_id_type=MESH,
        ).wait_recv()

    for target in [side] + deep + [twin]:
        push(0, me, target, tok)
    loads[0].wait()
    loads[1].wait()
    turned = contract(nxt_in[...], order[...], 0)
    held_nxt[me] = jnp.concatenate([turned[:split], turned[split:]], axis=1).astype(KIND)
    for target in [side] + deep + [twin]:
        push(1, me, target)
    for target in [side] + deep + [twin]:
        push(2, me, target, cot)

    place = (lax.broadcasted_iota(jnp.int32, (half, chunk), 1) % TILE).astype(jnp.float32)

    def build(slab, which):
        offsets = strip_offsets(indices, which)
        columns = offsets.shape[1]
        for start in range(0, breadth, chunk):
            span = slice(start, start + chunk)
            where = dot(offsets, spread[:columns, span])
            odd = where >= TILE
            hot = jnp.where(jnp.where(odd, where - TILE, where) == place, 1.0, 0.0)
            waves = dot(hot.astype(KIND), across[...])
            basis[slab, :half, span] = jnp.where(odd, 0.0, waves).astype(KIND)
            basis[slab, half:, span] = jnp.where(odd, waves, 0.0).astype(KIND)

    def relay_deep(kinds):
        for kind in kinds:
            for which in deep:
                arrive(kind, which)
                push(kind, which, side)
                push(kind, which, twin)

    def relay_side(kinds):
        for kind in kinds:
            for zz in [z] + others:
                which = slot(zz, 1 - x, core)
                arrive(kind, which)
                push(kind, which, twin)

    for n in (2, 3):
        loads[n].wait()
    build(0, replica)
    relay_deep((0, 1))

    for k in range(1, replicas):
        build(k, (replica + k) % replicas)
    relay_side((0, 1))
    relay_deep((2,))

    for n in (4, 5, 6):
        loads[n].wait()
    wide_sum = upper_sum = None
    for zz in [z] + others:
        for kind in range(2):
            if zz is z:
                arrive(kind, twin)
            else:
                arrive(kind, slot(zz, x, 1 - core))
            arrive(kind, slot(zz, 1 - x, 1 - core))
        for n in range(4):
            base = n * share
            which = zz * 4 + n
            features[base : base + share, :count] = held_tok[which]
            features[base : base + split, count:] = held_nxt[which, :, :nexts]
            features[base + split : base + share, count:] = held_nxt[which, :, nexts:]
        turned = features[...].T
        at = pl.ds(pl.multiple_of(zz * group, 16), group)
        first, second = dot(turned, gate[at]), dot(turned, upper[at])
        wide_sum = first if wide_sum is None else wide_sum + first
        upper_sum = second if upper_sum is None else upper_sum + second
    mixed = (wide_sum / (1.0 + jnp.exp(-wide_sum)) * upper_sum).astype(KIND)
    relay_side((2,))
    tall = strip * TILE
    for n in range(rows // tall):
        hidden[n] = mixed[:count, n * tall : (n + 1) * tall]
    loads[8].wait()
    waved = dot(mixed, turn[...])
    rate = -STEP_RATE / replicas
    tops = waved[:count].astype(KIND).T
    tail = jnp.concatenate([mixed[count:], (waved[count:] * rate).astype(KIND)], axis=1)

    for n in (7, 9):
        loads[n].wait()
    tall = strip * TILE
    for n in range(rows // tall):
        low = n * tall // 2
        flat = slice(low, low + tall // 2)
        lower = slice(half + low, half + low + tall // 2)
        parts = []
        for start in range(0, breadth, chunk):
            span = slice(start, start + chunk)
            piece = momentum[n * tall : (n + 1) * tall, span]
            mixed = dot(row[...], jnp.concatenate([piece, piece], axis=0))
            parts.append(
                (
                    mixed[: tall // 2] * basis[0, flat, span].astype(jnp.float32)
                    + mixed[tall // 2 :] * basis[0, lower, span].astype(jnp.float32)
                ).astype(KIND)
            )
        early[flat] = dot(jnp.concatenate(parts, axis=1), gather[...])
    loads[10].wait()
    for zz in [z] + others:
        arrive(2, slot(zz, x, 1 - core))
        arrive(2, slot(zz, 1 - x, 1 - core))
    grads[...] = held_cot[...].reshape(breadth, count).T
    sums = early[...]
    for start in range(0, breadth, chunk):
        span = slice(start, start + chunk)
        lifted = dot(tops, grads[:, span])
        part = lifted[:half] * basis[0, :half, span].astype(jnp.float32) + lifted[
            half:
        ] * basis[0, half:, span].astype(jnp.float32)
        sums = sums + dot(part.astype(KIND), gather[span])
    values = sums.astype(KIND)
    mine[...] = sums.T[: mine.shape[0]].astype(KIND)

    def share_values(k):
        return pltpu.make_async_remote_copy(
            src_ref=mine,
            dst_ref=theirs.at[k - 1],
            send_sem=pass_send.at[k - 1],
            recv_sem=pass_recv.at[k - 1],
            device_id={"replica": (replica - k + replicas) % replicas},
            device_id_type=MESH,
        )

    for k in range(1, replicas):
        share_values(k).start()

    loads[11].wait()
    spans = [slice(start, start + wide) for start in range(0, breadth, wide)]
    for span in spans:
        spot = dot(values, spread[:, span])
        top = (spot * basis[0, :half, span].astype(jnp.float32)).astype(KIND)
        low = (spot * basis[0, half:, span].astype(jnp.float32)).astype(KIND)
        pair[0, :, span] = top
        pair[1, :, span] = low
        total[:, span] = dot(tail, jnp.concatenate([down[:, span], top, low], axis=0))
    for k in range(1, replicas):
        share_values(k).wait()
    blank = jnp.zeros((spread.shape[0] - mine.shape[0], half), jnp.float32)
    foreign = [
        jnp.concatenate([theirs[k].astype(jnp.float32), blank], axis=0).T.astype(KIND)
        for k in range(replicas - 1)
    ]

    quarter = nexts // 4
    short = nexts // size

    def fold_core(n):
        return pltpu.make_async_remote_copy(
            src_ref=stage_core.at[n], dst_ref=held_core.at[n],
            send_sem=fold_send.at[0, n], recv_sem=fold_recv.at[0, n],
            device_id={"tensor": twin}, device_id_type=MESH,
        )

    def fold_side(n):
        return pltpu.make_async_remote_copy(
            src_ref=stage_side.at[n], dst_ref=held_side.at[n],
            send_sem=fold_send.at[1, n], recv_sem=fold_recv.at[1, n],
            device_id={"tensor": side}, device_id_type=MESH,
        )

    def fold_deep(n, k):
        return pltpu.make_async_remote_copy(
            src_ref=stage_deep.at[n, others[k - 1]], dst_ref=held_deep.at[n, k - 1],
            send_sem=deep_send.at[n, k - 1], recv_sem=deep_recv.at[n, k - 1],
            device_id={"tensor": deep[k - 1]}, device_id_type=MESH,
        )

    def first_stage(n):
        span = spans[n]
        tops, lows = [], []
        for k in range(1, replicas):
            spot = dot(foreign[k - 1], spread[:, span])
            tops.append((spot * basis[k, :half, span].astype(jnp.float32)).astype(KIND))
            lows.append((spot * basis[k, half:, span].astype(jnp.float32)).astype(KIND))
        more = total[:, span]
        for top, low in zip(tops, lows):
            more = more + dot(tail[:, rows:], jnp.concatenate([top, low], axis=0))
        total[:, span] = more
        away = pl.ds(pl.multiple_of((1 - core) * 2 * quarter, 8), 2 * quarter)
        stage_core[n] = total[away, span].astype(KIND)
        fold_core(n).start()

    def second_stage(n):
        span = spans[n]
        fold_core(n).wait()
        base = core * 2 * quarter
        away = pl.ds(pl.multiple_of(base + (1 - x) * quarter, 8), quarter)
        here = pl.ds(pl.multiple_of(base + x * quarter, 8), quarter)
        got = pl.ds(pl.multiple_of((1 - x) * quarter, 8), quarter)
        left = pl.ds(pl.multiple_of(x * quarter, 8), quarter)
        stage_side[n] = (total[away, span] + held_core[n, got].astype(jnp.float32)).astype(KIND)
        fold_side(n).start()
        total[here, span] = total[here, span] + held_core[n, left].astype(jnp.float32)

    def third_stage(n):
        span = spans[n]
        fold_side(n).wait()
        base = core * 2 * quarter + x * quarter
        here = pl.ds(pl.multiple_of(base, 8), quarter)
        full = total[here, span] + held_side[n].astype(jnp.float32)
        for zz in range(depth):
            piece = full[zz * short : (zz + 1) * short]
            stage_deep[n, zz] = piece.astype(KIND)
            split_sum[n, zz] = piece
        for k in range(1, depth):
            fold_deep(n, k).start()

    steps = len(spans)
    lag, far = 2, 4
    for n in range(steps + far):
        if n < steps:
            first_stage(n)
        if 0 <= n - lag < steps:
            second_stage(n - lag)
        if 0 <= n - far:
            third_stage(n - far)
    for n in range(steps):
        span = spans[n]
        piece = split_sum[n, z]
        for k in range(1, depth):
            fold_deep(n, k).wait()
            piece = piece + held_deep[n, k - 1].astype(jnp.float32)
        out[:, span] = piece
    for copy in copies:
        copy.wait_send()


def step_pass(args, consts, size, replicas, strip, chunk, wide):
    tok, nxt, cot, gate, upper, down, momentum, indices = args
    share, count = tok.shape
    nexts = nxt.shape[0]
    rows, breadth = down.shape
    half = rows // 2
    depth = size // 4
    short = nexts // size
    columns = indices.shape[3]
    ribbon = columns + -columns % 128
    steps = breadth // wide
    quarter = nexts // 4
    pushes = 3 * (depth + 1 + 3 * depth - 2)

    def like(array):
        return pltpu.VMEM(array.shape, array.dtype)

    return pl.pallas_call(
        functools.partial(step_kernel, size, replicas, strip, chunk, wide),
        out_shape=(
            jax.ShapeDtypeStruct((short, breadth), jnp.float32),
            pltpu.VMEM((rows // (strip * TILE), count, strip * TILE), KIND),
            pltpu.VMEM((count, breadth), KIND),
            pltpu.VMEM((2, half, breadth), KIND),
            pltpu.VMEM((rows, breadth), KIND),
        ),
        in_specs=[ANY] * (len(args) + len(consts)),
        out_specs=(VMEM,) * 5,
        scratch_shapes=[
            like(nxt),
            pltpu.VMEM((size, share, count), KIND),
            pltpu.VMEM((size, share // 2, 2 * nexts), KIND),
            pltpu.VMEM((size, share, count), KIND),
            like(gate), like(upper), like(down), like(indices),
            pltpu.VMEM((ribbon, breadth), KIND),
            pltpu.VMEM((breadth, ribbon), KIND),
            *[like(const) for const in consts],
            pltpu.VMEM((4 * share, count + nexts), KIND),
            pltpu.VMEM((replicas, rows, breadth), KIND),
            pltpu.VMEM((half, ribbon), jnp.float32),
            pltpu.VMEM((columns, half), KIND),
            pltpu.VMEM((replicas - 1, columns, half), KIND),
            pltpu.VMEM((nexts, breadth), jnp.float32),
            pltpu.VMEM((steps, 2 * quarter, wide), KIND),
            pltpu.VMEM((steps, 2 * quarter, wide), KIND),
            pltpu.VMEM((steps, quarter, wide), KIND),
            pltpu.VMEM((steps, quarter, wide), KIND),
            pltpu.VMEM((steps, depth, short, wide), KIND),
            pltpu.VMEM((steps, depth - 1, short, wide), KIND),
            pltpu.VMEM((steps, depth, short, wide), jnp.float32),
            pltpu.SemaphoreType.DMA((pushes,)),
            pltpu.SemaphoreType.DMA((3, size)),
            pltpu.SemaphoreType.DMA((12,)),
            pltpu.SemaphoreType.DMA((replicas - 1,)),
            pltpu.SemaphoreType.DMA((replicas - 1,)),
            pltpu.SemaphoreType.DMA((2, steps)),
            pltpu.SemaphoreType.DMA((2, steps)),
            pltpu.SemaphoreType.DMA((steps, depth - 1)),
            pltpu.SemaphoreType.DMA((steps, depth - 1)),
        ],
        compiler_params=pltpu.CompilerParams(
            collective_id=0, has_side_effects=True, vmem_limit_bytes=44 * 2**20
        ),
        name="step_pass",
    )(*[pltpu.with_memory_space_constraint(array, pltpu.HBM) for array in [*args, *consts]])


def kept_kernel(tall, chunk, hidden, grads, momentum, pair, inverse, raw, kept, out):
    step = pl.program_id(0)
    breadth = grads.shape[1]
    low = pl.ds(pl.multiple_of(step * (tall // 2), 8), tall // 2)
    here = pl.ds(pl.multiple_of(step * tall, 8), tall)
    left = jnp.concatenate([hidden[step].T, inverse[...]], axis=1)
    for start in range(0, breadth, chunk):
        span = slice(start, start + chunk)
        right = jnp.concatenate([grads[:, span], pair[0, low, span], pair[1, low, span]], axis=0)
        kept[0, :, span] = (
            BETA_DECAY * momentum[here, span].astype(jnp.float32) + dot(left, right)
        ).astype(KIND)

    @pl.when(step == 0)
    def _():
        out[...] = raw[...].astype(KIND)


def whole_block(array):
    return pl.BlockSpec(array.shape, lambda i: (0,) * array.ndim)


def kept_pass(hidden, grads, momentum, pair, raw, strip, chunk):
    rows, breadth = momentum.shape
    tall = strip * TILE
    inverse = jnp.asarray(-halves(strip).T, jnp.float32).astype(KIND)
    return pl.pallas_call(
        functools.partial(kept_kernel, tall, chunk),
        grid=(rows // tall,),
        out_shape=(
            jax.ShapeDtypeStruct((1, rows, breadth), KIND),
            jax.ShapeDtypeStruct(raw.shape, KIND),
        ),
        in_specs=[VMEM, VMEM, VMEM, VMEM, whole_block(inverse), whole_block(raw)],
        out_specs=(
            pl.BlockSpec((1, tall, breadth), lambda i: (0, i, 0)),
            whole_block(raw),
        ),
        compiler_params=pltpu.CompilerParams(vmem_limit_bytes=24 * 2**20),
        name="kept_pass",
    )(hidden, grads, momentum, pair, inverse, raw)


def on_device(
    tokens, next_tokens, cotangent, gate_weight, up_weight, down_weight, momentum, indices
):
    size = lax.axis_size("tensor")
    replicas = lax.axis_size("replica")
    share = tokens.shape[1]
    nexts = next_tokens.shape[0]
    breadth = share * size
    tile_rows = indices.shape[1]
    strip = next(n for n in (2, 1) if tile_rows % n == 0)
    chunk = next(n for n in (256, 128) if breadth % n == 0)
    wide = 2 * chunk if breadth % (2 * chunk) == 0 else chunk

    high, low = split_bf16(BETA_DECAY * halves(strip))
    depth, short = size // 4, nexts // size
    order = np.zeros((nexts, nexts))
    for n in range(nexts):
        owner, rest = n // short, n % short
        z, x, core = owner // 4, (owner // 2) % 2, owner % 2
        order[n, ((core * 2 + x) * depth + z) * short + rest] = 1.0
    consts = [
        jnp.concatenate([high, low], axis=1),
        jnp.asarray(halves(tile_rows).T, jnp.float32).astype(KIND),
        jnp.asarray(np.kron(np.eye(chunk // TILE), cosine_table()), jnp.float32).astype(KIND),
        jnp.asarray(order, KIND),
    ]
    args = [
        tokens.T, next_tokens, cotangent.T, gate_weight, up_weight, down_weight, momentum,
        jnp.swapaxes(indices, 2, 3),
    ]
    raw, hidden, grads, pair, held = step_pass(args, consts, size, replicas, strip, chunk, wide)
    kept, output = kept_pass(hidden, grads, held, pair, raw, strip, chunk)
    return (output, kept)


def solution(mesh):
    return jax.shard_map(
        on_device,
        mesh=mesh,
        in_specs=(
            P("replica", "tensor"),
            P("replica", "tensor"),
            P("replica", "tensor"),
            P(None, "tensor"),
            P(None, "tensor"),
            P("tensor", None),
            P("replica", "tensor", None),
            P(None, "tensor", None, None),
        ),
        out_specs=(P(("replica", "tensor"), None), P("replica", "tensor", None)),
        check_vma=False,
    )
```

time: 65.4 us -> 50 us (0.76)
  Pallas kernels: 60.5 us -> 49.2 us
  local copies, waits for them, and re-layouts: 2.21 us -> 0.01 us
  other arithmetic: 1.49 us -> 0 us
    pallas_call x3 -> x2, Pallas kernels: 60.5 us -> 49.2 us  [the longest x1 44.3 us: step_pass(): pl.pallas_call(functools.partial(step_kernel, size, replicas, strip, chun...]
    unnamed x2, local copies, waits for them, and re-layouts: 2.21 us -> 0.01 us
    concatenate x1 -> x0, other arithmetic: 1.49 us -> none  [on_device(): jnp.concatenate([tokens.T, jnp.concatenate([turned[:share // 2], turned[s...]
where the time goes in v1:
time: 50 us; the launch traced here: 49.9 us
  Pallas kernels  49.2 us (98%)
  between operations  0.66 us (1%)
    pallas_call x1, Pallas kernels, step_pass(): pl.pallas_call(functools.partial(step_kernel, size, replicas, strip, chun...  44.3 us
    pallas_call x1, Pallas kernels, kept_pass(): pl.pallas_call(functools.partial(kept_kernel, tall, chunk), grid=(rows //...  4.85 us

profile of v1, /device:TPU:0, one launch (start us, length us, event | category | flops | bytes accessed | tf_op | source)
XLA Modules:
  0.0 49.9 jit_solution(7633178765080676888)
XLA Ops:
  0.6 0.0 copy-start
  0.6 44.3 %step_pass.1 = (f32[4,2560]{1,0:T(4,128)S(1)}, bf16[7,128,128]{2,1,0:T(8,128)(2,1)S(1)}, bf16[128,2560]{1,0:T(8,128)(2,1)S(1)}, bf16[2,448,2560]{2,1,0:T(8,128)(2,1)S(1)}, bf16[896,2560]{1,0:T(8,128)(2,1)S(1)}) custom-call(bf16[160,128]{1,0:T(8,128)(2,1)} %bitcast.4, bf16[64,160]{1,0:T(8,128)(2,1)} %nxt.1, bf16[160,128]{1,0:T(8,128)(2,1)} %bitcast.5, ...), custom_call_target="tpu_custom_call" | custom-call | tf_op jit(solution)/shard_map/step_pass/pallas_call | solution.py:396
  45.0 0.0 copy-done
  45.0 4.8 %kept_pass.1 = (bf16[1,896,2560]{2,1,0:T(8,128)(2,1)}, bf16[4,2560]{1,0:T(4,128)(2,1)}) custom-call(bf16[7,128,128]{2,1,0:T(8,128)(2,1)S(1)} %get-tuple-element.9.hidden, bf16[128,2560]{1,0:T(8,128)(2,1)S(1)} %get-tuple-element.10.grads, bf16[896,2560]{1,0:T(8,128)(2,1)S(1)} %get-tuple-element.11.momentum, bf16[2,448,2560]{2,1,0:T(8,128)(2,1)S(1)} %get-tuple-element.12.pair, ...), custom_call_target="tpu_custom_call" | custom-call | tf_op jit(solution)/shard_map/kept_pass/pallas_call | solution.py:472
Async XLA Ops:
  0.6 44.4 %copy-start = (bf16[128,128]{1,0:T(8,128)(2,1)S(1)}, bf16[128,128]{1,0:T(8,128)(2,1)}, u32[]{:S(2)}) copy-start(bf16[128,128]{1,0:T(8,128)(2,1)} %constant.24.inverse) | copy-start | bytes 98308

commit v2 on v1

--- a/solution.py
+++ b/solution.py
@@ -67,11 +67,11 @@
 def step_kernel(
     size, replicas, strip, chunk, wide,
     tok, nxt, cot, gate_hbm, upper_hbm, down_hbm, momentum_hbm, indices_hbm,
-    row_hbm, turn_hbm, across_hbm, order_hbm,
-    out, hidden, grads, pair, momentum,
+    row_hbm, turn_hbm, across_hbm, order_hbm, inverse_hbm,
+    out, momentum,
     nxt_in, held_tok, held_nxt, held_cot,
-    gate, upper, down, indices, spread, gather, row, turn, across, order,
-    features, basis, early, mine, theirs, total,
+    gate, upper, down, indices, spread, gather, row, turn, across, order, inverse,
+    features, basis, early, hidden, grads, pair, mine, theirs, total,
     stage_core, held_core, stage_side, held_side, stage_deep, held_deep, split_sum,
     send, recv, local, pass_send, pass_recv, fold_send, fold_recv, deep_send, deep_recv,
 ):
@@ -94,6 +94,7 @@
         (nxt, nxt_in), (order_hbm, order), (indices_hbm, indices), (across_hbm, across),
         (tok, held_tok.at[me]), (gate_hbm, gate), (upper_hbm, upper), (row_hbm, row),
         (turn_hbm, turn), (momentum_hbm.at[0], momentum), (cot, held_cot.at[me]), (down_hbm, down),
+        (inverse_hbm, inverse),
     ]
     loads = [
         pltpu.make_async_copy(source, target, local.at[n])
@@ -146,54 +147,92 @@
             device_id_type=MESH,
         ).wait_recv()
 
-    for target in [side] + deep + [twin]:
+    for target in deep + [side, twin]:
         push(0, me, target, tok)
     loads[0].wait()
     loads[1].wait()
     turned = contract(nxt_in[...], order[...], 0)
     held_nxt[me] = jnp.concatenate([turned[:split], turned[split:]], axis=1).astype(KIND)
-    for target in [side] + deep + [twin]:
+    for target in deep + [side, twin]:
         push(1, me, target)
-    for target in [side] + deep + [twin]:
+    for target in deep:
         push(2, me, target, cot)
 
     place = (lax.broadcasted_iota(jnp.int32, (half, chunk), 1) % TILE).astype(jnp.float32)
 
-    def build(slab, which):
-        offsets = strip_offsets(indices, which)
-        columns = offsets.shape[1]
-        for start in range(0, breadth, chunk):
-            span = slice(start, start + chunk)
-            where = dot(offsets, spread[:columns, span])
-            odd = where >= TILE
-            hot = jnp.where(jnp.where(odd, where - TILE, where) == place, 1.0, 0.0)
-            waves = dot(hot.astype(KIND), across[...])
-            basis[slab, :half, span] = jnp.where(odd, 0.0, waves).astype(KIND)
-            basis[slab, half:, span] = jnp.where(odd, waves, 0.0).astype(KIND)
-
-    def relay_deep(kinds):
-        for kind in kinds:
-            for which in deep:
-                arrive(kind, which)
-                push(kind, which, side)
-                push(kind, which, twin)
-
-    def relay_side(kinds):
-        for kind in kinds:
-            for zz in [z] + others:
-                which = slot(zz, 1 - x, core)
-                arrive(kind, which)
-                push(kind, which, twin)
+    def build(slab, offsets, span):
+        where = dot(offsets, spread[: offsets.shape[1], span])
+        odd = where >= TILE
+        hot = jnp.where(jnp.where(odd, where - TILE, where) == place, 1.0, 0.0)
+        waves = dot(hot.astype(KIND), across[...])
+        basis[slab, :half, span] = jnp.where(odd, 0.0, waves).astype(KIND)
+        basis[slab, half:, span] = jnp.where(odd, waves, 0.0).astype(KIND)
+
+    def from_deep(kind, which):
+        arrive(kind, which)
+        push(kind, which, side)
+        push(kind, which, twin)
+
+    def from_side(kind, zz):
+        which = slot(zz, 1 - x, core)
+        arrive(kind, which)
+        push(kind, which, twin)
+
+    def send_late():
+        for target in (side, twin):
+            push(2, me, target, cot)
+
+    def drain(events, most):
+        for _ in range(min(most, len(events))):
+            events.pop(0)()
+
+    bind = functools.partial
+    first_events = []
+    for kind in range(2):
+        first_events.append(bind(from_side, kind, z))
+        first_events += [bind(from_deep, kind, which) for which in deep]
+    first_events.append(send_late)
+    for kind in range(2):
+        first_events += [bind(from_side, kind, zz) for zz in others]
+    last_events = [bind(from_deep, 2, which) for which in deep]
+    last_events += [bind(from_side, 2, zz) for zz in [z] + others]
+
+    narrow = [slice(start, start + chunk) for start in range(0, breadth, chunk)]
+    tall = strip * TILE
+
+    def spectrum(n):
+        low = n * tall // 2
+        flat = slice(low, low + tall // 2)
+        lower = slice(half + low, half + low + tall // 2)
+        parts = []
+        for span in narrow:
+            piece = momentum[n * tall : (n + 1) * tall, span]
+            mixed = dot(row[...], jnp.concatenate([piece, piece], axis=0))
+            parts.append(
+                (
+                    mixed[: tall // 2] * basis[0, flat, span].astype(jnp.float32)
+                    + mixed[tall // 2 :] * basis[0, lower, span].astype(jnp.float32)
+                ).astype(KIND)
+            )
+        early[flat] = dot(jnp.concatenate(parts, axis=1), gather[...])
 
     for n in (2, 3):
         loads[n].wait()
-    build(0, replica)
-    relay_deep((0, 1))
-
+    offsets = strip_offsets(indices, replica)
+    for span in narrow:
+        build(0, offsets, span)
     for k in range(1, replicas):
-        build(k, (replica + k) % replicas)
-    relay_side((0, 1))
-    relay_deep((2,))
+        offsets = strip_offsets(indices, (replica + k) % replicas)
+        for span in narrow:
+            build(k, offsets, span)
+            drain(first_events, 1)
+    for n in (7, 9):
+        loads[n].wait()
+    strips = list(range(rows // tall))
+    while first_events:
+        if len(strips) > 4:
+            spectrum(strips.pop(0))
+        drain(first_events, 2)
 
     for n in (4, 5, 6):
         loads[n].wait()
@@ -216,9 +255,9 @@
         first, second = dot(turned, gate[at]), dot(turned, upper[at])
         wide_sum = first if wide_sum is None else wide_sum + first
         upper_sum = second if upper_sum is None else upper_sum + second
+        drain(last_events, 1)
     mixed = (wide_sum / (1.0 + jnp.exp(-wide_sum)) * upper_sum).astype(KIND)
-    relay_side((2,))
-    tall = strip * TILE
+    drain(last_events, 1)
     for n in range(rows // tall):
         hidden[n] = mixed[:count, n * tall : (n + 1) * tall]
     loads[8].wait()
@@ -227,25 +266,10 @@
     tops = waved[:count].astype(KIND).T
     tail = jnp.concatenate([mixed[count:], (waved[count:] * rate).astype(KIND)], axis=1)
 
-    for n in (7, 9):
-        loads[n].wait()
-    tall = strip * TILE
-    for n in range(rows // tall):
-        low = n * tall // 2
-        flat = slice(low, low + tall // 2)
-        lower = slice(half + low, half + low + tall // 2)
-        parts = []
-        for start in range(0, breadth, chunk):
-            span = slice(start, start + chunk)
-            piece = momentum[n * tall : (n + 1) * tall, span]
-            mixed = dot(row[...], jnp.concatenate([piece, piece], axis=0))
-            parts.append(
-                (
-                    mixed[: tall // 2] * basis[0, flat, span].astype(jnp.float32)
-                    + mixed[tall // 2 :] * basis[0, lower, span].astype(jnp.float32)
-                ).astype(KIND)
-            )
-        early[flat] = dot(jnp.concatenate(parts, axis=1), gather[...])
+    while strips or last_events:
+        if strips:
+            spectrum(strips.pop(0))
+        drain(last_events, 1)
     loads[10].wait()
     for zz in [z] + others:
         arrive(2, slot(zz, x, 1 - core))
@@ -356,6 +380,18 @@
         for k in range(1, depth):
             fold_deep(n, k).start()
 
+    def remain(n):
+        rows_here = slice(n * tall, (n + 1) * tall)
+        low = slice(n * tall // 2, (n + 1) * tall // 2)
+        left = jnp.concatenate([hidden[n].T, inverse[...]], axis=1)
+        for span in narrow:
+            right = jnp.concatenate([grads[:, span], pair[0, low, span], pair[1, low, span]], axis=0)
+            momentum[rows_here, span] = (
+                BETA_DECAY * momentum[rows_here, span].astype(jnp.float32) + dot(left, right)
+            ).astype(KIND)
+
+    loads[12].wait()
+    strips = list(range(rows // tall))
     steps = len(spans)
     lag, far = 2, 4
     for n in range(steps + far):
@@ -365,6 +401,12 @@
             second_stage(n - lag)
         if 0 <= n - far:
             third_stage(n - far)
+        if n >= steps:
+            for _ in range(1 if n == steps else 2):
+                if strips:
+                    remain(strips.pop(0))
+    while strips:
+        remain(strips.pop(0))
     for n in range(steps):
         span = spans[n]
         piece = split_sum[n, z]
@@ -396,14 +438,11 @@
     return pl.pallas_call(
         functools.partial(step_kernel, size, replicas, strip, chunk, wide),
         out_shape=(
-            jax.ShapeDtypeStruct((short, breadth), jnp.float32),
-            pltpu.VMEM((rows // (strip * TILE), count, strip * TILE), KIND),
-            pltpu.VMEM((count, breadth), KIND),
-            pltpu.VMEM((2, half, breadth), KIND),
+            pltpu.VMEM((short, breadth), jnp.float32),
             pltpu.VMEM((rows, breadth), KIND),
         ),
         in_specs=[ANY] * (len(args) + len(consts)),
-        out_specs=(VMEM,) * 5,
+        out_specs=(VMEM,) * 2,
         scratch_shapes=[
             like(nxt),
             pltpu.VMEM((size, share, count), KIND),
@@ -416,6 +455,9 @@
             pltpu.VMEM((4 * share, count + nexts), KIND),
             pltpu.VMEM((replicas, rows, breadth), KIND),
             pltpu.VMEM((half, ribbon), jnp.float32),
+            pltpu.VMEM((rows // (strip * TILE), count, strip * TILE), KIND),
+            pltpu.VMEM((count, breadth), KIND),
+            pltpu.VMEM((2, half, breadth), KIND),
             pltpu.VMEM((columns, half), KIND),
             pltpu.VMEM((replicas - 1, columns, half), KIND),
             pltpu.VMEM((nexts, breadth), jnp.float32),
@@ -428,7 +470,7 @@
             pltpu.VMEM((steps, depth, short, wide), jnp.float32),
             pltpu.SemaphoreType.DMA((pushes,)),
             pltpu.SemaphoreType.DMA((3, size)),
-            pltpu.SemaphoreType.DMA((12,)),
+            pltpu.SemaphoreType.DMA((13,)),
             pltpu.SemaphoreType.DMA((replicas - 1,)),
             pltpu.SemaphoreType.DMA((replicas - 1,)),
             pltpu.SemaphoreType.DMA((2, steps)),
@@ -437,53 +479,40 @@
             pltpu.SemaphoreType.DMA((steps, depth - 1)),
         ],
         compiler_params=pltpu.CompilerParams(
-            collective_id=0, has_side_effects=True, vmem_limit_bytes=44 * 2**20
+            collective_id=0, has_side_effects=True, vmem_limit_bytes=52 * 2**20
         ),
         name="step_pass",
     )(*[pltpu.with_memory_space_constraint(array, pltpu.HBM) for array in [*args, *consts]])
 
 
-def kept_kernel(tall, chunk, hidden, grads, momentum, pair, inverse, raw, kept, out):
-    step = pl.program_id(0)
-    breadth = grads.shape[1]
-    low = pl.ds(pl.multiple_of(step * (tall // 2), 8), tall // 2)
-    here = pl.ds(pl.multiple_of(step * tall, 8), tall)
-    left = jnp.concatenate([hidden[step].T, inverse[...]], axis=1)
-    for start in range(0, breadth, chunk):
-        span = slice(start, start + chunk)
-        right = jnp.concatenate([grads[:, span], pair[0, low, span], pair[1, low, span]], axis=0)
-        kept[0, :, span] = (
-            BETA_DECAY * momentum[here, span].astype(jnp.float32) + dot(left, right)
-        ).astype(KIND)
-
-    @pl.when(step == 0)
-    def _():
-        out[...] = raw[...].astype(KIND)
-
-
-def whole_block(array):
-    return pl.BlockSpec(array.shape, lambda i: (0,) * array.ndim)
-
-
-def kept_pass(hidden, grads, momentum, pair, raw, strip, chunk):
-    rows, breadth = momentum.shape
-    tall = strip * TILE
-    inverse = jnp.asarray(-halves(strip).T, jnp.float32).astype(KIND)
+def leave_kernel(parts, ready, raw, kept, out, sems):
+    tall = ready.shape[0] // parts
+    copies = [
+        pltpu.make_async_copy(
+            ready.at[n * tall : (n + 1) * tall], kept.at[0, n * tall : (n + 1) * tall], sems.at[n]
+        )
+        for n in range(parts)
+    ]
+    for copy in copies:
+        copy.start()
+    out[...] = raw[...].astype(KIND)
+    for copy in copies:
+        copy.wait()
+
+
+def leave_pass(ready, raw, parts):
     return pl.pallas_call(
-        functools.partial(kept_kernel, tall, chunk),
-        grid=(rows // tall,),
+        functools.partial(leave_kernel, parts),
         out_shape=(
-            jax.ShapeDtypeStruct((1, rows, breadth), KIND),
+            jax.ShapeDtypeStruct((1,) + ready.shape, KIND),
             jax.ShapeDtypeStruct(raw.shape, KIND),
         ),
-        in_specs=[VMEM, VMEM, VMEM, VMEM, whole_block(inverse), whole_block(raw)],
-        out_specs=(
-            pl.BlockSpec((1, tall, breadth), lambda i: (0, i, 0)),
-            whole_block(raw),
-        ),
-        compiler_params=pltpu.CompilerParams(vmem_limit_bytes=24 * 2**20),
-        name="kept_pass",
-    )(hidden, grads, momentum, pair, inverse, raw)
+        in_specs=[VMEM, VMEM],
+        out_specs=(ANY, VMEM),
+        scratch_shapes=[pltpu.SemaphoreType.DMA((parts,))],
+        compiler_params=pltpu.CompilerParams(vmem_limit_bytes=8 * 2**20),
+        name="leave_pass",
+    )(ready, raw)
 
 
 def on_device(
@@ -511,13 +540,14 @@
         jnp.asarray(halves(tile_rows).T, jnp.float32).astype(KIND),
         jnp.asarray(np.kron(np.eye(chunk // TILE), cosine_table()), jnp.float32).astype(KIND),
         jnp.asarray(order, KIND),
+        jnp.asarray(-halves(strip).T, jnp.float32).astype(KIND),
     ]
     args = [
         tokens.T, next_tokens, cotangent.T, gate_weight, up_weight, down_weight, momentum,
         jnp.swapaxes(indices, 2, 3),
     ]
-    raw, hidden, grads, pair, held = step_pass(args, consts, size, replicas, strip, chunk, wide)
-    kept, output = kept_pass(hidden, grads, held, pair, raw, strip, chunk)
+    raw, ready = step_pass(args, consts, size, replicas, strip, chunk, wide)
+    kept, output = leave_pass(ready, raw, 7)
     return (output, kept)
 
 

time: 50 us -> 48 us (0.960)
  Pallas kernels: 49.2 us -> 47 us
    pallas_call x1, Pallas kernels: 4.85 us -> 2.8 us  [leave_pass(): pl.pallas_call(functools.partial(leave_kernel, parts), out_shape=(jax.Sha...]
where the time goes in v2:
time: 48 us; the launch traced here: 47.8 us
  Pallas kernels  47 us (98%)
  between operations  0.8 us (2%)
    pallas_call x1, Pallas kernels, step_pass(): pl.pallas_call(functools.partial(step_kernel, size, replicas, strip, chun...  44.2 us
    pallas_call x1, Pallas kernels, leave_pass(): pl.pallas_call(functools.partial(leave_kernel, parts), out_shape=(jax.Sha...  2.8 us

profile of v2, /device:TPU:0, one launch (start us, length us, event | category | flops | bytes accessed | tf_op | source)
XLA Modules:
  0.0 47.8 jit_solution(5993556133937224578)
XLA Ops:
  0.6 44.2 %step_pass.1 = (f32[4,2560]{1,0:T(4,128)S(1)}, bf16[896,2560]{1,0:T(8,128)(2,1)S(1)}) custom-call(bf16[160,128]{1,0:T(8,128)(2,1)} %bitcast.4, bf16[64,160]{1,0:T(8,128)(2,1)} %nxt.1, bf16[160,128]{1,0:T(8,128)(2,1)} %bitcast.5, bf16[2560,896]{1,0:T(8,128)(2,1)} %gate_hbm.1, bf16[2560,896]{1,0:T(8,128)(2,1)} %upper_hbm.1, bf16[896,2560]{1,0:T(8,128)(2,1)} %down_hbm.1, ...), custom_call_target="tpu_custom_call" | custom-call | tf_op jit(solution)/shard_map/step_pass/pallas_call | solution.py:438
  44.9 2.8 %leave_pass.1 = (bf16[1,896,2560]{2,1,0:T(8,128)(2,1)}, bf16[4,2560]{1,0:T(4,128)(2,1)}) custom-call(bf16[896,2560]{1,0:T(8,128)(2,1)S(1)} %get-tuple-element.6.ready, f32[4,2560]{1,0:T(4,128)S(1)} %get-tuple-element.7.raw), custom_call_target="tpu_custom_call" | custom-call | tf_op jit(solution)/shard_map/leave_pass/pallas_call | solution.py:504
